TPU v7x, 32 devices: a whole 2x2x4 slice. The times are simulated.
32 devices in a mesh: cluster: 16 (over z, y, x), ens: 2 (over core).
Axes of the slice: x: 2, y: 2, z: 4, core: 2. Of those that a mesh axis runs over, the one named last changes fastest.
Arguments:
- log_rate: float32 [16, 16384], P('ens', 'cluster'), may hold values from -1 to 0.5
- state: float32 [16, 16384], P('ens', 'cluster'), may hold values from -1 to 1
- rate_coef: float32 [16, 16384], P('ens', 'cluster'), may hold values from 0.5 to 2
- state_coef: float32 [16, 16384], P('ens', 'cluster'), may hold values from 0.5 to 2
- near_weight: bfloat16 [3, 16384, 1024], P(None, 'cluster', 'ens'), may hold values from -0.21582031 to 0.21582031
- col_basis: bfloat16 [64, 16384], P(None, 'cluster'), may hold values from -0.1875 to 0.1875
- coupling: float32 [1024, 1024], P('cluster'), may hold values from -0.1875 to 0.1875
- cluster_row_factors: float32 [64, 16384], P(None, 'cluster'), may hold values from -2.25 to 2.25
- ranks: int32 [16], P('cluster'), may hold values from 16 to 64, as said below
Outputs:
- log_rate_next: float32 [16, 16384], P('ens', 'cluster')
- state_next: float32 [16, 16384], P('ens', 'cluster')
Inputs may be any that keep to these rules, and one draw needn't show every extreme that they name: `ranks`: each cluster's rank lies in 16 to 64; some cluster has rank 64.
All inputs are finite; a program needn't handle non-finite values.
Results may differ from a plain program's by a relative error of at most 0.0017.
Values may be sent and summed in bfloat16 or wider, within the bound.
A program may use at most 64 MiB of HBM per device.

v0:
```python
import functools

import jax
import jax.numpy as jnp
from jax import lax
from jax.experimental import pallas as pl
from jax.experimental.pallas import tpu as pltpu
from jax.sharding import PartitionSpec as P

step_length = 0.5
damping = 0.5

MESH = pl.DeviceIdType.MESH
ROWS = (((1,), (1,)), ((), ()))


def split(value):
    high = value.astype(jnp.bfloat16)
    low = (value - high.astype(jnp.float32)).astype(jnp.bfloat16)
    return high, low


def kernel(
    n,
    log_rate_hbm,
    state_hbm,
    rate_coef_hbm,
    state_coef_hbm,
    near_hbm,
    basis_hbm,
    coupling_hbm,
    factors_hbm,
    ranks_hbm,
    sums_out,
    ranks_ref,
    log_rate_ref,
    state_ref,
    rate_coef_ref,
    state_coef_ref,
    near_ref,
    basis_ref,
    coupling_ref,
    factors_ref,
    far_in,
    far_out,
    halves,
    halo,
    coef_send,
    coef_recv,
    part_send,
    part_recv,
    load_sem,
    halo_send_sem,
    halo_recv_sem,
    coef_send_sem,
    coef_recv_sem,
    part_send_sem,
    part_recv_sem,
):
    me = lax.axis_index("cluster")
    core = lax.axis_index("ens")
    other = 1 - core
    members, rows = log_rate_ref.shape
    half = rows // 2
    widest = basis_ref.shape[0]

    loads = [
        pltpu.make_async_copy(source, target, load_sem.at[i])
        for i, (source, target) in enumerate(
            (
                (log_rate_hbm, log_rate_ref),
                (basis_hbm, basis_ref),
                (state_hbm, state_ref),
                (coupling_hbm, coupling_ref),
                (factors_hbm, factors_ref),
                (near_hbm, near_ref),
                (rate_coef_hbm, rate_coef_ref),
                (state_coef_hbm, state_coef_ref),
                (ranks_hbm, ranks_ref),
            )
        )
    ]
    for i in (0, 1, 8, 2, 3, 4, 5, 6, 7):
        loads[i].start()

    barrier = pltpu.get_barrier_semaphore()

    def greet(cluster, ens):
        pl.semaphore_signal(barrier, inc=1, device_id=(cluster, ens), device_id_type=MESH)

    for d in range(1, n):
        greet(lax.rem(me + d, n), core)
    greet(me, other)

    @pl.when(me > 0)
    def _():
        greet(me - 1, other)

    @pl.when(me < n - 1)
    def _():
        greet(me + 1, other)

    lane = lax.broadcasted_iota(jnp.int32, (members, 2 * widest), 1)
    lane_rank = lax.rem(lane, widest)

    zero_coef = jnp.zeros((members, 2 * widest), coef_recv.dtype)
    zero_half = jnp.zeros((members, half), halo.dtype)
    for section in range(2):
        coef_recv[section, me] = zero_coef

        @pl.when(me > 0)
        def _():
            coef_recv[section, jnp.maximum(me - 1, 0)] = zero_coef

        @pl.when(me < n - 1)
        def _():
            coef_recv[section, jnp.minimum(me + 1, n - 1)] = zero_coef

        @pl.when(me == 0)
        def _():
            for slot in range(2):
                halo[section, 0, slot] = zero_half

        @pl.when(me == n - 1)
        def _():
            for slot in range(2):
                halo[section, 2, slot] = zero_half

    def halo_copy(section, k, slot, cluster):
        ens = core if slot == 0 else other
        return pltpu.make_async_remote_copy(
            src_ref=halves.at[section, ens],
            dst_ref=halo.at[section, k, slot],
            send_sem=halo_send_sem.at[section, k, slot],
            recv_sem=halo_recv_sem.at[section, k, slot],
            device_id=(cluster, ens),
            device_id_type=MESH,
        )

    def coef_copy(section, cluster):
        return pltpu.make_async_remote_copy(
            src_ref=coef_send.at[section],
            dst_ref=coef_recv.at[section, me],
            send_sem=coef_send_sem.at[section, cluster],
            recv_sem=coef_recv_sem.at[section, me],
            device_id=(cluster, core),
            device_id_type=MESH,
        )

    def coef_arrival(section, cluster):
        return pltpu.make_async_remote_copy(
            src_ref=coef_send.at[section],
            dst_ref=coef_recv.at[section, cluster],
            send_sem=coef_send_sem.at[section, cluster],
            recv_sem=coef_recv_sem.at[section, cluster],
            device_id=(cluster, core),
            device_id_type=MESH,
        )

    def part_copy(section):
        return pltpu.make_async_remote_copy(
            src_ref=part_send.at[section],
            dst_ref=part_recv.at[section],
            send_sem=part_send_sem.at[section],
            recv_sem=part_recv_sem.at[section],
            device_id=(me, other),
            device_id_type=MESH,
        )

    def each_far(action):
        for d in sorted(range(2, n - 1), key=lambda d: abs(2 * d - n)):
            action(lax.rem(me + d, n))

        @pl.when(me == 0)
        def _():
            action(jnp.int32(n - 1))

        @pl.when(me == n - 1)
        def _():
            action(jnp.int32(0))

    def prepare(own_rank):
        loads[3].wait()
        row = lax.broadcasted_iota(jnp.int32, (widest, 2 * widest), 0)
        kept = row < own_rank
        for j in range(n):
            block = coupling_ref[:, j * widest : (j + 1) * widest]
            block = jnp.concatenate([block, block], axis=1)
            block = jnp.where(jnp.logical_and(kept, jnp.abs(me - j) > 1), block, 0.0)
            high, low = split(block)
            far_in[0:widest, 2 * j * widest : 2 * (j + 1) * widest] = high
            far_in[widest : 2 * widest, 2 * j * widest : 2 * (j + 1) * widest] = low
        loads[4].wait()
        high, low = split(factors_ref[...])
        far_out[0:widest] = high
        far_out[widest : 2 * widest] = high
        far_out[2 * widest : 3 * widest] = low
        far_out[3 * widest : 4 * widest] = low

    def rates(section, current_logarithm, own_rank):
        rate = jnp.exp(current_logarithm)
        deficit = (rate - 1.0).astype(jnp.bfloat16)
        halves[section, 0] = deficit[:, :half]
        halves[section, 1] = deficit[:, half:]
        halo[section, 1, 0] = halves[section, core]
        basis = basis_ref[...]
        coef = lax.dot_general(
            deficit,
            jnp.concatenate([basis, basis], axis=0),
            ROWS,
            preferred_element_type=jnp.float32,
        )
        coef = jnp.where(lane_rank < own_rank, coef, 0.0)
        high = coef.astype(jnp.bfloat16).astype(jnp.float32)
        coef_send[section] = jnp.where(lane < widest, high, coef - high).astype(jnp.bfloat16)

        if section == 0:
            greeted = n + jnp.where(me > 0, 1, 0) + jnp.where(me < n - 1, 1, 0)
            pl.semaphore_wait(barrier, greeted)

        each_far(lambda cluster: coef_copy(section, cluster).start())

        @pl.when(me > 0)
        def _():
            for slot in range(2):
                halo_copy(section, 2, slot, me - 1).start()

        @pl.when(me < n - 1)
        def _():
            for slot in range(2):
                halo_copy(section, 0, slot, me + 1).start()

        halo_copy(section, 1, 1, me).start()

        if section == 0:
            prepare(own_rank)
            loads[5].wait()

        def near(k):
            columns = jnp.concatenate([halo[section, k, 0], halo[section, k, 1]], axis=0)
            return lax.dot_general(
                columns, near_ref[k], ROWS, preferred_element_type=jnp.float32
            )

        halo_copy(section, 1, 1, me).wait_recv()
        total = near(1)

        @pl.when(me > 0)
        def _():
            for slot in range(2):
                halo_copy(section, 0, slot, me - 1).wait_recv()

        total = total + near(0)

        @pl.when(me < n - 1)
        def _():
            for slot in range(2):
                halo_copy(section, 2, slot, me + 1).wait_recv()

        total = total + near(2)
        part_send[section] = total[members:]
        part_copy(section).start()

        each_far(lambda cluster: coef_arrival(section, cluster).wait_recv())
        coefs = jnp.concatenate([coef_recv[section, j] for j in range(n)], axis=1)
        reduced = lax.dot_general(coefs, far_in[...], ROWS, preferred_element_type=jnp.float32)
        high, low = split(reduced)
        reduced = jnp.concatenate(
            [jnp.concatenate([high, high], axis=1), jnp.concatenate([low, low], axis=1)], axis=0
        )
        far = jnp.dot(reduced, far_out[...], preferred_element_type=jnp.float32)
        stress_rate = total[:members] + (far[:members] + far[members:])
        part_copy(section).wait_recv()
        return rate, stress_rate + part_recv[section]

    loads[0].wait()
    loads[1].wait()
    loads[8].wait()
    own_rank = ranks_ref[0]
    log_rate = log_rate_ref[...]
    rate, stress_one = rates(0, log_rate, own_rank)
    loads[2].wait()
    loads[6].wait()
    loads[7].wait()
    state = state_ref[...]
    rate_coef = rate_coef_ref[...]
    state_coef = state_coef_ref[...]
    state_one = jnp.exp(-state) - rate
    rate_one = (stress_one - state_coef * state_one) / (rate_coef + damping * rate)
    second, stress_two = rates(1, log_rate + step_length * rate_one, own_rank)
    state_two = jnp.exp(-(state + step_length * state_one)) - second
    rate_two = (stress_two - state_coef * state_two) / (rate_coef + damping * second)
    sums_out[0] = rate_one + rate_two
    sums_out[1] = state_one + state_two

    for section in range(2):
        each_far(lambda cluster: coef_copy(section, cluster).wait_send())

        @pl.when(me > 0)
        def _():
            for slot in range(2):
                halo_copy(section, 2, slot, me - 1).wait_send()

        @pl.when(me < n - 1)
        def _():
            for slot in range(2):
                halo_copy(section, 0, slot, me + 1).wait_send()

        halo_copy(section, 1, 1, me).wait_send()
        part_copy(section).wait_send()


def finish(sums_ref, log_rate_ref, state_ref, log_rate_out, state_out):
    log_rate_out[...] = log_rate_ref[...] + 0.5 * step_length * sums_ref[0]
    state_out[...] = state_ref[...] + 0.5 * step_length * sums_ref[1]


def local(n, *args):
    log_rate, near_weight, col_basis, coupling, factors = (args[i] for i in (0, 4, 5, 6, 7))
    members, rows = log_rate.shape
    half = near_weight.shape[2]
    widest = col_basis.shape[0]
    f32, bf16 = jnp.float32, jnp.bfloat16
    in_hbm = pl.BlockSpec(memory_space=pltpu.HBM)
    vmem = pl.BlockSpec(memory_space=pltpu.VMEM)
    sums = pl.pallas_call(
            functools.partial(kernel, n),
            out_shape=pltpu.VMEM((2, members, rows), f32),
            in_specs=[in_hbm] * 9,
            out_specs=vmem,
            scratch_shapes=[
                pltpu.SMEM((1,), jnp.int32),
                pltpu.VMEM((members, rows), f32),
                pltpu.VMEM((members, rows), f32),
                pltpu.VMEM((members, rows), f32),
                pltpu.VMEM((members, rows), f32),
                pltpu.VMEM(near_weight.shape, bf16),
                pltpu.VMEM(col_basis.shape, bf16),
                pltpu.VMEM(coupling.shape, f32),
                pltpu.VMEM(factors.shape, f32),
                pltpu.VMEM((2 * widest, n * 2 * widest), bf16),
                pltpu.VMEM((4 * widest, rows), bf16),
                pltpu.VMEM((2, 2, members, half), bf16),
                pltpu.VMEM((2, 3, 2, members, half), bf16),
                pltpu.VMEM((2, members, 2 * widest), bf16),
                pltpu.VMEM((2, n, members, 2 * widest), bf16),
                pltpu.VMEM((2, members, rows), f32),
                pltpu.VMEM((2, members, rows), f32),
                pltpu.SemaphoreType.DMA((9,)),
                pltpu.SemaphoreType.DMA((2, 3, 2)),
                pltpu.SemaphoreType.DMA((2, 3, 2)),
                pltpu.SemaphoreType.DMA((2, n)),
                pltpu.SemaphoreType.DMA((2, n)),
                pltpu.SemaphoreType.DMA((2,)),
                pltpu.SemaphoreType.DMA((2,)),
            ],
            compiler_params=pltpu.CompilerParams(
                collective_id=0, has_side_effects=True, vmem_limit_bytes=60 * 1024 * 1024
            ),
        )(*args)
    return tuple(
        pl.pallas_call(
            finish,
            out_shape=[jax.ShapeDtypeStruct((members, rows), f32)] * 2,
            in_specs=[vmem] * 3,
            out_specs=[vmem] * 2,
            compiler_params=pltpu.CompilerParams(vmem_limit_bytes=1024 * 1024),
        )(sums, args[0], args[1])
    )


def solution(mesh):
    in_specs = (
        P("ens", "cluster"),
        P("ens", "cluster"),
        P("ens", "cluster"),
        P("ens", "cluster"),
        P(None, "cluster", "ens"),
        P(None, "cluster"),
        P("cluster", None),
        P(None, "cluster"),
        P("cluster"),
    )
    out_specs = (P("ens", "cluster"), P("ens", "cluster"))
    return jax.shard_map(
        functools.partial(local, mesh.shape["cluster"]),
        mesh=mesh,
        in_specs=in_specs,
        out_specs=out_specs,
        check_vma=False,
    )
```

profile of v0, /device:TPU:0, one launch (start us, length us, event | category | flops | bytes accessed | tf_op | source)
XLA Modules:
  0.0 20.6 jit_solution(4221563532954556434)
XLA Ops:
  0.6 0.0 copy-start.1
  0.6 0.0 copy-start
  1.3 18.7 %shard_map.104.sums_ref = f32[2,8,1024]{2,1,0:T(8,128)S(1)} custom-call(f32[8,1024]{1,0:T(8,128)} %log_rate_ref.1, f32[8,1024]{1,0:T(8,128)} %state_ref.1, f32[8,1024]{1,0:T(8,128)} %rate_coef_hbm.1, f32[8,1024]{1,0:T(8,128)} %state_coef_hbm.1, bf16[3,1024,512]{2,1,0:T(8,128)(2,1)} %near_hbm.1, bf16[64,1024]{1,0:T(8,128)(2,1)} %basis_hbm.1, ...), custom_call_target="tpu_custom_call" | custom-call | tf_op jit(solution)/shard_map/pallas_call | solution.py:326
  20.0 0.0 copy-done.1
  20.0 0.0 copy-done
  20.0 0.6 %shard_map.105 = (f32[8,1024]{1,0:T(8,128)}, f32[8,1024]{1,0:T(8,128)}) custom-call(f32[2,8,1024]{2,1,0:T(8,128)S(1)} %shard_map.104.sums_ref, f32[8,1024]{1,0:T(8,128)S(1)} %copy-done, f32[8,1024]{1,0:T(8,128)S(1)} %copy-done.1), custom_call_target="tpu_custom_call" | custom-call | tf_op jit(solution)/shard_map/pallas_call | solution.py:362
Async XLA Ops:
  0.6 19.4 %copy-start.1 = (f32[8,1024]{1,0:T(8,128)S(1)}, f32[8,1024]{1,0:T(8,128)}, u32[]{:S(2)}) copy-start(f32[8,1024]{1,0:T(8,128)} %state_ref.1) | copy-start | bytes 98308
  0.6 19.4 %copy-start = (f32[8,1024]{1,0:T(8,128)S(1)}, f32[8,1024]{1,0:T(8,128)}, u32[]{:S(2)}) copy-start(f32[8,1024]{1,0:T(8,128)} %log_rate_ref.1) | copy-start | bytes 98308
where the time goes:
time: 20.8 us; the launch traced here: 20.6 us
  Pallas kernels  19.3 us (93%)
  between operations  1.33 us (6%)
    pallas_call x1, Pallas kernels, local(): pl.pallas_call(functools.partial(kernel, n), out_shape=pltpu.VMEM((2, mem...  18.7 us
    pallas_call x1, Pallas kernels, local(): pl.pallas_call(finish, out_shape=[jax.ShapeDtypeStruct((members, rows), f...  0.63 us

commit v1 on v0

v1 whole, which is shorter than its diff:
```python
import functools
import math

import jax
import jax.numpy as jnp
from jax import lax
from jax.experimental import pallas as pl
from jax.experimental.pallas import tpu as pltpu
from jax.sharding import PartitionSpec as P

step_length = 0.5
damping = 0.5

MESH = pl.DeviceIdType.MESH
ROWS = (((1,), (1,)), ((), ()))


def split(value):
    high = value.astype(jnp.bfloat16)
    low = (value - high.astype(jnp.float32)).astype(jnp.bfloat16)
    return high, low


def kernel(
    n,
    group,
    log_rate_hbm,
    state_hbm,
    rate_coef_hbm,
    state_coef_hbm,
    near_hbm,
    basis_hbm,
    coupling_hbm,
    factors_hbm,
    ranks_ref,
    sums_out,
    log_rate_ref,
    basis_ref,
    friction,
    near_ref,
    coupling_ref,
    factors_ref,
    far_in,
    far_out,
    halves,
    halo,
    coef,
    part_send,
    part_recv,
    load_sem,
    upper_sem,
    halo_send_sem,
    partner_send_sem,
    halo_recv_sem,
    coef_send_sem,
    coef_recv_sem,
    part_recv_sem,
):
    me = lax.axis_index("cluster")
    core = lax.axis_index("ens")
    other = 1 - core
    levels = n // group
    level = me // group
    place = me % group
    members, rows = log_rate_ref.shape
    half = rows // 2
    widest = basis_ref.shape[0]

    barrier = pltpu.get_barrier_semaphore()

    def greet(cluster, ens):
        pl.semaphore_signal(barrier, inc=1, device_id=(cluster, ens), device_id_type=MESH)

    for d in range(1, group):
        greet(level * group + (place + d) % group, core)
    greet(me, other)

    @pl.when(me > 0)
    def _():
        greet(me - 1, other)

    @pl.when(me < n - 1)
    def _():
        greet(me + 1, other)

    @pl.when(jnp.logical_and(place == 0, level > 0))
    def _():
        greet(me - 1, core)

    for d in range(1, levels):

        @pl.when(level + d < levels)
        def _():
            for p in range(group):
                greet((level + d) * group + p, core)

    loads = [
        pltpu.make_async_copy(source, target, load_sem.at[i])
        for i, (source, target) in enumerate(
            (
                (log_rate_hbm, log_rate_ref),
                (basis_hbm, basis_ref),
                (coupling_hbm, coupling_ref),
                (factors_hbm, factors_ref),
                (near_hbm, near_ref),
            )
        )
    ]
    for load in loads:
        load.start()
    for i, source in enumerate((state_hbm, rate_coef_hbm, state_coef_hbm)):
        pltpu.make_async_copy(source, friction.at[i], load_sem.at[len(loads)]).start()

    own_rank = ranks_ref[0]
    lane = lax.broadcasted_iota(jnp.int32, (members, 2 * widest), 1)
    lane_rank = lax.rem(lane, widest)

    zero_half = jnp.zeros((members, half), halo.dtype)
    for section in range(2):

        @pl.when(me == 0)
        def _():
            for slot in range(2):
                halo[section, 0, slot] = zero_half

        @pl.when(me == n - 1)
        def _():
            for slot in range(2):
                halo[section, 2, slot] = zero_half

    def halo_copy(section, k, slot, cluster):
        ens = core if slot == 0 else other
        return pltpu.make_async_remote_copy(
            src_ref=halves.at[section, ens],
            dst_ref=halo.at[section, k, slot],
            send_sem=partner_send_sem if k == 1 else halo_send_sem.at[k // 2],
            recv_sem=halo_recv_sem.at[section, k],
            device_id=(cluster, ens),
            device_id_type=MESH,
        )

    def halo_arrival(section, k):
        return pltpu.make_async_remote_copy(
            src_ref=halo.at[section, k],
            dst_ref=halo.at[section, k],
            send_sem=halo_send_sem.at[k // 2],
            recv_sem=halo_recv_sem.at[section, k],
            device_id=(me, other),
            device_id_type=MESH,
        )

    def coef_copy(section, first, count, cluster):
        return pltpu.make_async_remote_copy(
            src_ref=coef.at[section, pl.ds(first, count)],
            dst_ref=coef.at[section, pl.ds(first, count)],
            send_sem=coef_send_sem,
            recv_sem=coef_recv_sem.at[section, level],
            device_id=(cluster, core),
            device_id_type=MESH,
        )

    def coef_arrival(section, source, count):
        return pltpu.make_async_remote_copy(
            src_ref=coef.at[section, pl.ds(source * group, count)],
            dst_ref=coef.at[section, pl.ds(source * group, count)],
            send_sem=coef_send_sem,
            recv_sem=coef_recv_sem.at[section, source],
            device_id=(me, other),
            device_id_type=MESH,
        )

    def part_copy(section):
        return pltpu.make_async_remote_copy(
            src_ref=part_send.at[section],
            dst_ref=part_recv.at[section],
            send_sem=partner_send_sem,
            recv_sem=part_recv_sem.at[section],
            device_id=(me, other),
            device_id_type=MESH,
        )

    def prepare():
        loads[2].wait()
        row = lax.broadcasted_iota(jnp.int32, (widest, 2 * widest), 0)
        kept = row < own_rank
        for j in range(n):
            block = coupling_ref[:, j * widest : (j + 1) * widest]
            block = jnp.concatenate([block, block], axis=1)
            block = jnp.where(jnp.logical_and(kept, jnp.abs(me - j) > 1), block, 0.0)
            high, low = split(block)
            columns = slice(2 * (j % group) * widest, 2 * (j % group + 1) * widest)
            far_in[j // group, 0:widest, columns] = high
            far_in[j // group, widest : 2 * widest, columns] = low
        loads[3].wait()
        high, low = split(factors_ref[...])
        far_out[0:widest] = high
        far_out[widest : 2 * widest] = high
        far_out[2 * widest : 3 * widest] = low
        far_out[3 * widest : 4 * widest] = low

    turn = jnp.where(2 * level < levels, 1, levels - 1)

    def rates(section, current_logarithm):
        rate = jnp.exp(current_logarithm)
        deficit = (rate - 1.0).astype(jnp.bfloat16)
        halves[section, 0] = deficit[:, :half]
        halves[section, 1] = deficit[:, half:]
        halo[section, 1, 0] = halves[section, core]
        if section == 0:
            loads[1].wait()
        basis = basis_ref[...]
        own = lax.dot_general(
            deficit,
            jnp.concatenate([basis, basis], axis=0),
            ROWS,
            preferred_element_type=jnp.float32,
        )
        own = jnp.where(lane_rank < own_rank, own, 0.0)
        high = own.astype(jnp.bfloat16).astype(jnp.float32)
        coef[section, me] = jnp.where(lane < widest, high, own - high).astype(jnp.bfloat16)

        if section == 0:
            greeted = (
                group * (level + 1)
                + jnp.where(me > 0, 1, 0)
                + jnp.where(me < n - 1, 1, 0)
                + jnp.where(jnp.logical_and(place == group - 1, level < levels - 1), 1, 0)
            )
            pl.semaphore_wait(barrier, greeted)

            for d in range(levels - 1, 0, -1):

                @pl.when(level >= d)
                def _():
                    pl.semaphore_signal(
                        upper_sem,
                        inc=1,
                        device_id=((level - d) * group + place, core),
                        device_id_type=MESH,
                    )

            for d in range(levels - 1, 0, -1):

                @pl.when(level >= d)
                def _():
                    for p in range(group):
                        coef_copy(section, me, 1, (level - d) * group + p).start()

            for d in range(1, group):
                coef_copy(section, me, 1, level * group + (place + d) % group).start()
        else:
            for j in range(n):

                @pl.when(j != me)
                def _():
                    coef_copy(section, me, 1, jnp.int32(j)).start()

        @pl.when(me > 0)
        def _():
            for slot in range(2):
                halo_copy(section, 2, slot, me - 1).start()

        @pl.when(me < n - 1)
        def _():
            for slot in range(2):
                halo_copy(section, 0, slot, me + 1).start()

        halo_copy(section, 1, 1, me).start()

        if section == 0:
            prepare()
            loads[4].wait()

        def near(k):
            columns = jnp.concatenate([halo[section, k, 0], halo[section, k, 1]], axis=0)
            return lax.dot_general(
                columns, near_ref[k], ROWS, preferred_element_type=jnp.float32
            )

        if section == 0:
            @pl.when(level < levels - 1)
            def _():
                coef_arrival(section, level, group - 1).wait_recv()
                pl.semaphore_wait(upper_sem, levels - 1 - level)
                for d in range(levels - 1, 0, -1):

                    @pl.when(level + d < levels)
                    def _():
                        coef_copy(
                            section, level * group, group, (level + d) * group + place
                        ).start()

        halo_copy(section, 1, 1, me).wait_recv()
        total = near(1)

        @pl.when(me > 0)
        def _():
            halo_arrival(section, 0).wait_recv()

        total = total + near(0)

        @pl.when(me < n - 1)
        def _():
            halo_arrival(section, 2).wait_recv()

        total = total + near(2)
        part_send[section] = total[members:]
        part_copy(section).start()

        if section == 0:

            @pl.when(level == levels - 1)
            def _():
                coef_arrival(section, level, group - 1).wait_recv()
        else:
            coef_arrival(section, level, group - 1).wait_recv()

        reduced = None
        for d in range(levels):
            source = (level + d * turn) % levels
            if d > 0:
                coef_arrival(section, source, group).wait_recv()
            coefs = coef[section, pl.ds(source * group, group)]
            coefs = jnp.concatenate([coefs[j] for j in range(group)], axis=1)
            term = lax.dot_general(
                coefs, far_in[source], ROWS, preferred_element_type=jnp.float32
            )
            reduced = term if reduced is None else reduced + term
        high, low = split(reduced)
        reduced = jnp.concatenate(
            [jnp.concatenate([high, high], axis=1), jnp.concatenate([low, low], axis=1)], axis=0
        )
        far = jnp.dot(reduced, far_out[...], preferred_element_type=jnp.float32)
        stress_rate = total[:members] + (far[:members] + far[members:])
        part_copy(section).wait_recv()
        return rate, stress_rate + part_recv[section]

    loads[0].wait()
    log_rate = log_rate_ref[...]
    rate, stress_one = rates(0, log_rate)
    pltpu.make_async_copy(friction, friction, load_sem.at[len(loads)]).wait()
    state, rate_coef, state_coef = friction[0], friction[1], friction[2]
    state_one = jnp.exp(-state) - rate
    rate_one = (stress_one - state_coef * state_one) / (rate_coef + damping * rate)
    second, stress_two = rates(1, log_rate + step_length * rate_one)
    state_two = jnp.exp(-(state + step_length * state_one)) - second
    rate_two = (stress_two - state_coef * state_two) / (rate_coef + damping * second)
    sums_out[0] = rate_one + rate_two
    sums_out[1] = state_one + state_two

    def sent(source, semaphore):
        pltpu.make_async_remote_copy(
            src_ref=source,
            dst_ref=source,
            send_sem=semaphore,
            recv_sem=part_recv_sem.at[0],
            device_id=(me, other),
            device_id_type=MESH,
        ).wait_send()

    sent(coef.at[:, pl.ds(0, n - 1)], coef_send_sem)

    @pl.when(me > 0)
    def _():
        sent(halves, halo_send_sem.at[1])

    @pl.when(me < n - 1)
    def _():
        sent(halves, halo_send_sem.at[0])

    for section in range(2):
        halo_copy(section, 1, 1, me).wait_send()
        part_copy(section).wait_send()


def finish(sums_ref, log_rate_ref, state_ref, log_rate_out, state_out):
    log_rate_out[...] = log_rate_ref[...] + 0.5 * step_length * sums_ref[0]
    state_out[...] = state_ref[...] + 0.5 * step_length * sums_ref[1]


def local(n, *args):
    log_rate, near_weight, col_basis, coupling, factors = (args[i] for i in (0, 4, 5, 6, 7))
    members, rows = log_rate.shape
    half = near_weight.shape[2]
    widest = col_basis.shape[0]
    group = max(d for d in range(1, math.isqrt(n) + 1) if n % d == 0)
    levels = n // group
    f32, bf16 = jnp.float32, jnp.bfloat16
    in_hbm = pl.BlockSpec(memory_space=pltpu.HBM)
    vmem = pl.BlockSpec(memory_space=pltpu.VMEM)
    smem = pl.BlockSpec(memory_space=pltpu.SMEM)
    sums = pl.pallas_call(
        functools.partial(kernel, n, group),
        out_shape=pltpu.VMEM((2, members, rows), f32),
        in_specs=[in_hbm] * 8 + [smem],
        out_specs=vmem,
        scratch_shapes=[
            pltpu.VMEM((members, rows), f32),
            pltpu.VMEM(col_basis.shape, bf16),
            pltpu.VMEM((3, members, rows), f32),
            pltpu.VMEM(near_weight.shape, bf16),
            pltpu.VMEM(coupling.shape, f32),
            pltpu.VMEM(factors.shape, f32),
            pltpu.VMEM((levels, 2 * widest, group * 2 * widest), bf16),
            pltpu.VMEM((4 * widest, rows), bf16),
            pltpu.VMEM((2, 2, members, half), bf16),
            pltpu.VMEM((2, 3, 2, members, half), bf16),
            pltpu.VMEM((2, n, members, 2 * widest), bf16),
            pltpu.VMEM((2, members, rows), f32),
            pltpu.VMEM((2, members, rows), f32),
            pltpu.SemaphoreType.DMA((6,)),
            pltpu.SemaphoreType.REGULAR,
            pltpu.SemaphoreType.DMA((2,)),
            pltpu.SemaphoreType.DMA,
            pltpu.SemaphoreType.DMA((2, 3)),
            pltpu.SemaphoreType.DMA,
            pltpu.SemaphoreType.DMA((2, levels)),
            pltpu.SemaphoreType.DMA((2,)),
        ],
        compiler_params=pltpu.CompilerParams(
            collective_id=0, has_side_effects=True, vmem_limit_bytes=60 * 1024 * 1024
        ),
    )(*args)
    return tuple(
        pl.pallas_call(
            finish,
            out_shape=[jax.ShapeDtypeStruct((members, rows), f32)] * 2,
            in_specs=[vmem] * 3,
            out_specs=[vmem] * 2,
            compiler_params=pltpu.CompilerParams(vmem_limit_bytes=1024 * 1024),
        )(sums, args[0], args[1])
    )


def solution(mesh):
    in_specs = (
        P("ens", "cluster"),
        P("ens", "cluster"),
        P("ens", "cluster"),
        P("ens", "cluster"),
        P(None, "cluster", "ens"),
        P(None, "cluster"),
        P("cluster", None),
        P(None, "cluster"),
        P("cluster"),
    )
    out_specs = (P("ens", "cluster"), P("ens", "cluster"))
    return jax.shard_map(
        functools.partial(local, mesh.shape["cluster"]),
        mesh=mesh,
        in_specs=in_specs,
        out_specs=out_specs,
        check_vma=False,
    )
```

time: 20.8 us -> 18.8 us (0.904)
  Pallas kernels: 19.3 us -> 17.3 us
    pallas_call x1, Pallas kernels: 18.7 us -> 16.7 us  [local(): pl.pallas_call(functools.partial(kernel, n, group), out_shape=pltpu.VMEM(...]
where the time goes in v1:
time: 18.8 us; the launch traced here: 18.7 us
  Pallas kernels  17.3 us (92%)
  between operations  1.33 us (7%)
    pallas_call x1, Pallas kernels, local(): pl.pallas_call(functools.partial(kernel, n, group), out_shape=pltpu.VMEM(...  16.7 us
    pallas_call x1, Pallas kernels, local(): pl.pallas_call(finish, out_shape=[jax.ShapeDtypeStruct((members, rows), f...  0.63 us

profile of v1, /device:TPU:0, one launch (start us, length us, event | category | flops | bytes accessed | tf_op | source)
XLA Modules:
  0.0 18.7 jit_solution(13076762592450951036)
XLA Ops:
  0.6 0.0 copy-start.1
  0.6 0.0 copy-start
  1.3 16.7 %shard_map.104.sums_ref = f32[2,8,1024]{2,1,0:T(8,128)S(1)} custom-call(f32[8,1024]{1,0:T(8,128)} %log_rate_ref.1, f32[8,1024]{1,0:T(8,128)} %state_ref.1, f32[8,1024]{1,0:T(8,128)} %rate_coef_hbm.1, f32[8,1024]{1,0:T(8,128)} %state_coef_hbm.1, bf16[3,1024,512]{2,1,0:T(8,128)(2,1)} %near_hbm.1, bf16[64,1024]{1,0:T(8,128)(2,1)} %basis_hbm.1, ...), custom_call_target="tpu_custom_call" | custom-call | tf_op jit(solution)/shard_map/pallas_call | solution.py:392
  18.0 0.0 copy-done.1
  18.0 0.0 copy-done
  18.0 0.6 %shard_map.105 = (f32[8,1024]{1,0:T(8,128)}, f32[8,1024]{1,0:T(8,128)}) custom-call(f32[2,8,1024]{2,1,0:T(8,128)S(1)} %shard_map.104.sums_ref, f32[8,1024]{1,0:T(8,128)S(1)} %copy-done, f32[8,1024]{1,0:T(8,128)S(1)} %copy-done.1), custom_call_target="tpu_custom_call" | custom-call | tf_op jit(solution)/shard_map/pallas_call | solution.py:425
Async XLA Ops:
  0.6 17.4 %copy-start.1 = (f32[8,1024]{1,0:T(8,128)S(1)}, f32[8,1024]{1,0:T(8,128)}, u32[]{:S(2)}) copy-start(f32[8,1024]{1,0:T(8,128)} %state_ref.1) | copy-start | bytes 98308
  0.6 17.4 %copy-start = (f32[8,1024]{1,0:T(8,128)S(1)}, f32[8,1024]{1,0:T(8,128)}, u32[]{:S(2)}) copy-start(f32[8,1024]{1,0:T(8,128)} %log_rate_ref.1) | copy-start | bytes 98308

commit v2 on v1

--- a/solution.py
+++ b/solution.py
@@ -40,6 +40,7 @@
     near_ref,
     coupling_ref,
     factors_ref,
+    basis_turned,
     far_in,
     far_out,
     halves,
@@ -48,11 +49,10 @@
     part_send,
     part_recv,
     load_sem,
+    last_sem,
     upper_sem,
-    halo_send_sem,
-    partner_send_sem,
+    send_sem,
     halo_recv_sem,
-    coef_send_sem,
     coef_recv_sem,
     part_recv_sem,
 ):
@@ -94,22 +94,27 @@
             for p in range(group):
                 greet((level + d) * group + p, core)
 
-    loads = [
-        pltpu.make_async_copy(source, target, load_sem.at[i])
-        for i, (source, target) in enumerate(
-            (
-                (log_rate_hbm, log_rate_ref),
-                (basis_hbm, basis_ref),
-                (coupling_hbm, coupling_ref),
-                (factors_hbm, factors_ref),
-                (near_hbm, near_ref),
-            )
-        )
-    ]
-    for load in loads:
-        load.start()
-    for i, source in enumerate((state_hbm, rate_coef_hbm, state_coef_hbm)):
-        pltpu.make_async_copy(source, friction.at[i], load_sem.at[len(loads)]).start()
+    def of_bytes(count):
+        tiles = count // (16 * 128)
+        across = next(c for c in (1, 2, 4) if tiles % c == 0 and 8 * tiles // c <= near_ref.shape[0])
+        return near_ref.at[pl.ds(0, 8 * tiles // across), pl.ds(0, 128 * across)]
+
+    loads = (
+        (log_rate_hbm, log_rate_ref, 0),
+        (basis_hbm, basis_ref, 0),
+        (coupling_hbm, coupling_ref, 1),
+        (factors_hbm, factors_ref, 1),
+        (state_hbm, friction.at[0], 1),
+        (rate_coef_hbm, friction.at[1], 1),
+        (state_coef_hbm, friction.at[2], 1),
+        (near_hbm, near_ref, 2),
+    )
+    for source, target, i in loads:
+        pltpu.make_async_copy(source, target, load_sem.at[i]).start()
+
+    def loaded(i):
+        count = sum(math.prod(t.shape) * t.dtype.itemsize for _, t, j in loads if i == j)
+        pltpu.make_async_copy(of_bytes(count), of_bytes(count), load_sem.at[i]).wait()
 
     own_rank = ranks_ref[0]
     lane = lax.broadcasted_iota(jnp.int32, (members, 2 * widest), 1)
@@ -133,7 +138,7 @@
         return pltpu.make_async_remote_copy(
             src_ref=halves.at[section, ens],
             dst_ref=halo.at[section, k, slot],
-            send_sem=partner_send_sem if k == 1 else halo_send_sem.at[k // 2],
+            send_sem=send_sem,
             recv_sem=halo_recv_sem.at[section, k],
             device_id=(cluster, ens),
             device_id_type=MESH,
@@ -143,7 +148,7 @@
         return pltpu.make_async_remote_copy(
             src_ref=halo.at[section, k],
             dst_ref=halo.at[section, k],
-            send_sem=halo_send_sem.at[k // 2],
+            send_sem=send_sem,
             recv_sem=halo_recv_sem.at[section, k],
             device_id=(me, other),
             device_id_type=MESH,
@@ -153,7 +158,7 @@
         return pltpu.make_async_remote_copy(
             src_ref=coef.at[section, pl.ds(first, count)],
             dst_ref=coef.at[section, pl.ds(first, count)],
-            send_sem=coef_send_sem,
+            send_sem=send_sem,
             recv_sem=coef_recv_sem.at[section, level],
             device_id=(cluster, core),
             device_id_type=MESH,
@@ -163,7 +168,7 @@
         return pltpu.make_async_remote_copy(
             src_ref=coef.at[section, pl.ds(source * group, count)],
             dst_ref=coef.at[section, pl.ds(source * group, count)],
-            send_sem=coef_send_sem,
+            send_sem=send_sem,
             recv_sem=coef_recv_sem.at[section, source],
             device_id=(me, other),
             device_id_type=MESH,
@@ -173,25 +178,28 @@
         return pltpu.make_async_remote_copy(
             src_ref=part_send.at[section],
             dst_ref=part_recv.at[section],
-            send_sem=partner_send_sem,
+            send_sem=send_sem,
             recv_sem=part_recv_sem.at[section],
             device_id=(me, other),
             device_id_type=MESH,
         )
 
     def prepare():
-        loads[2].wait()
-        row = lax.broadcasted_iota(jnp.int32, (widest, 2 * widest), 0)
-        kept = row < own_rank
-        for j in range(n):
-            block = coupling_ref[:, j * widest : (j + 1) * widest]
-            block = jnp.concatenate([block, block], axis=1)
-            block = jnp.where(jnp.logical_and(kept, jnp.abs(me - j) > 1), block, 0.0)
-            high, low = split(block)
-            columns = slice(2 * (j % group) * widest, 2 * (j % group + 1) * widest)
-            far_in[j // group, 0:widest, columns] = high
-            far_in[j // group, widest : 2 * widest, columns] = low
-        loads[3].wait()
+        turned = jnp.transpose(basis_ref[...].astype(jnp.float32)).astype(jnp.bfloat16)
+        basis_turned[...] = jnp.concatenate([turned, turned], axis=1)
+        loaded(1)
+        row = lax.broadcasted_iota(jnp.int32, (widest, group * widest), 0)
+        cluster = lax.broadcasted_iota(jnp.int32, (widest, group * widest), 1) // widest
+        for source in range(levels):
+            block = coupling_ref[:, source * group * widest : (source + 1) * group * widest]
+            far = jnp.abs(me - source * group - cluster) > 1
+            block = jnp.where(jnp.logical_and(row < own_rank, far), block, 0.0)
+            high, low = split(jnp.transpose(block))
+            block = jnp.concatenate([high, low], axis=1)
+            for j in range(group):
+                piece = block[j * widest : (j + 1) * widest]
+                far_in[source, 2 * j * widest : (2 * j + 1) * widest] = piece
+                far_in[source, (2 * j + 1) * widest : 2 * (j + 1) * widest] = piece
         high, low = split(factors_ref[...])
         far_out[0:widest] = high
         far_out[widest : 2 * widest] = high
@@ -200,44 +208,54 @@
 
     turn = jnp.where(2 * level < levels, 1, levels - 1)
 
-    def rates(section, current_logarithm):
+    def enter():
+        greeted = (
+            group * (level + 1)
+            + jnp.where(me > 0, 1, 0)
+            + jnp.where(me < n - 1, 1, 0)
+            + jnp.where(jnp.logical_and(place == group - 1, level < levels - 1), 1, 0)
+        )
+        pl.semaphore_wait(barrier, greeted)
+
+        def answer(semaphore, cluster):
+            pl.semaphore_signal(semaphore, inc=1, device_id=(cluster, core), device_id_type=MESH)
+
+        for d in range(levels - 1, 0, -1):
+
+            @pl.when(level >= d if d > 1 else jnp.logical_and(level > 0, level < levels - 1))
+            def _():
+                answer(upper_sem, (level - d) * group + place)
+
+        @pl.when(level == levels - 1)
+        def _():
+            for d in range(group):
+                answer(last_sem, (level - 1) * group + (place + d) % group)
+
+    def rates(section, current_logarithm, early):
         rate = jnp.exp(current_logarithm)
         deficit = (rate - 1.0).astype(jnp.bfloat16)
         halves[section, 0] = deficit[:, :half]
         halves[section, 1] = deficit[:, half:]
         halo[section, 1, 0] = halves[section, core]
         if section == 0:
-            loads[1].wait()
-        basis = basis_ref[...]
-        own = lax.dot_general(
-            deficit,
-            jnp.concatenate([basis, basis], axis=0),
-            ROWS,
-            preferred_element_type=jnp.float32,
-        )
+            basis = basis_ref[...]
+            own = lax.dot_general(
+                deficit,
+                jnp.concatenate([basis, basis], axis=0),
+                ROWS,
+                preferred_element_type=jnp.float32,
+            )
+        else:
+            own = jnp.dot(deficit, basis_turned[...], preferred_element_type=jnp.float32)
         own = jnp.where(lane_rank < own_rank, own, 0.0)
         high = own.astype(jnp.bfloat16).astype(jnp.float32)
         coef[section, me] = jnp.where(lane < widest, high, own - high).astype(jnp.bfloat16)
 
         if section == 0:
-            greeted = (
-                group * (level + 1)
-                + jnp.where(me > 0, 1, 0)
-                + jnp.where(me < n - 1, 1, 0)
-                + jnp.where(jnp.logical_and(place == group - 1, level < levels - 1), 1, 0)
-            )
-            pl.semaphore_wait(barrier, greeted)
-
-            for d in range(levels - 1, 0, -1):
-
-                @pl.when(level >= d)
-                def _():
-                    pl.semaphore_signal(
-                        upper_sem,
-                        inc=1,
-                        device_id=((level - d) * group + place, core),
-                        device_id_type=MESH,
-                    )
+
+            @pl.when(me < n - 1)
+            def _():
+                enter()
 
             for d in range(levels - 1, 0, -1):
 
@@ -269,16 +287,22 @@
 
         if section == 0:
             prepare()
-            loads[4].wait()
+            loaded(2)
 
         def near(k):
             columns = jnp.concatenate([halo[section, k, 0], halo[section, k, 1]], axis=0)
             return lax.dot_general(
-                columns, near_ref[k], ROWS, preferred_element_type=jnp.float32
+                columns, near_ref[k * rows : (k + 1) * rows], ROWS, preferred_element_type=jnp.float32
             )
 
         if section == 0:
-            @pl.when(level < levels - 1)
+            @pl.when(level == levels - 2)
+            def _():
+                pl.semaphore_wait(last_sem, group)
+                for d in range(group):
+                    coef_copy(section, me, 1, (level + 1) * group + (place + d) % group).start()
+
+            @pl.when(level < levels - 2)
             def _():
                 coef_arrival(section, level, group - 1).wait_recv()
                 pl.semaphore_wait(upper_sem, levels - 1 - level)
@@ -306,10 +330,11 @@
         total = total + near(2)
         part_send[section] = total[members:]
         part_copy(section).start()
+        early = early(rate)
 
         if section == 0:
 
-            @pl.when(level == levels - 1)
+            @pl.when(level >= levels - 2)
             def _():
                 coef_arrival(section, level, group - 1).wait_recv()
         else:
@@ -318,59 +343,65 @@
         reduced = None
         for d in range(levels):
             source = (level + d * turn) % levels
+            if section == 0 and d > 1:
+                source = jnp.where(level == levels - 1, d - 2, source)
             if d > 0:
                 coef_arrival(section, source, group).wait_recv()
             coefs = coef[section, pl.ds(source * group, group)]
             coefs = jnp.concatenate([coefs[j] for j in range(group)], axis=1)
-            term = lax.dot_general(
-                coefs, far_in[source], ROWS, preferred_element_type=jnp.float32
-            )
+            term = jnp.dot(coefs, far_in[source], preferred_element_type=jnp.float32)
             reduced = term if reduced is None else reduced + term
         high, low = split(reduced)
         reduced = jnp.concatenate(
             [jnp.concatenate([high, high], axis=1), jnp.concatenate([low, low], axis=1)], axis=0
         )
-        far = jnp.dot(reduced, far_out[...], preferred_element_type=jnp.float32)
+        far = jnp.concatenate(
+            [
+                jnp.dot(reduced, far_out[:, :half], preferred_element_type=jnp.float32),
+                jnp.dot(reduced, far_out[:, half:], preferred_element_type=jnp.float32),
+            ],
+            axis=1,
+        )
         stress_rate = total[:members] + (far[:members] + far[members:])
         part_copy(section).wait_recv()
-        return rate, stress_rate + part_recv[section]
-
-    loads[0].wait()
+        return stress_rate + part_recv[section], early
+
+    @pl.when(me == n - 1)
+    def _():
+        enter()
+
+    loaded(0)
     log_rate = log_rate_ref[...]
-    rate, stress_one = rates(0, log_rate)
-    pltpu.make_async_copy(friction, friction, load_sem.at[len(loads)]).wait()
-    state, rate_coef, state_coef = friction[0], friction[1], friction[2]
-    state_one = jnp.exp(-state) - rate
-    rate_one = (stress_one - state_coef * state_one) / (rate_coef + damping * rate)
-    second, stress_two = rates(1, log_rate + step_length * rate_one)
-    state_two = jnp.exp(-(state + step_length * state_one)) - second
-    rate_two = (stress_two - state_coef * state_two) / (rate_coef + damping * second)
-    sums_out[0] = rate_one + rate_two
+
+    def apart(rate, state, state_coef, rate_coef):
+        state_rate = jnp.exp(-state) - rate
+        return state_rate, state_coef * state_rate, 1.0 / (rate_coef + damping * rate)
+
+    def early_one(rate):
+        return apart(rate, friction[0], friction[2], friction[1])
+
+    stress_one, (state_one, healing, inverse) = rates(0, log_rate, early_one)
+    rate_one = (stress_one - healing) * inverse
+
+    def early_two(rate):
+        return apart(rate, friction[0] + step_length * state_one, friction[2], friction[1])
+
+    stress_two, (state_two, healing, inverse) = rates(
+        1, log_rate + step_length * rate_one, early_two
+    )
+    sums_out[0] = rate_one + (stress_two - healing) * inverse
     sums_out[1] = state_one + state_two
 
-    def sent(source, semaphore):
-        pltpu.make_async_remote_copy(
-            src_ref=source,
-            dst_ref=source,
-            send_sem=semaphore,
-            recv_sem=part_recv_sem.at[0],
-            device_id=(me, other),
-            device_id_type=MESH,
-        ).wait_send()
-
-    sent(coef.at[:, pl.ds(0, n - 1)], coef_send_sem)
-
-    @pl.when(me > 0)
-    def _():
-        sent(halves, halo_send_sem.at[1])
-
-    @pl.when(me < n - 1)
-    def _():
-        sent(halves, halo_send_sem.at[0])
-
-    for section in range(2):
-        halo_copy(section, 1, 1, me).wait_send()
-        part_copy(section).wait_send()
+    sent = 2 * (n - 1) * members * 2 * widest * 2 + 2 * (members * half * 2 + members * rows * 4)
+    side = 2 * 2 * members * half * 2
+
+    @pl.when(jnp.logical_and(me > 0, me < n - 1))
+    def _():
+        pltpu.make_async_copy(of_bytes(sent + 2 * side), of_bytes(sent + 2 * side), send_sem).wait()
+
+    @pl.when(jnp.logical_or(me == 0, me == n - 1))
+    def _():
+        pltpu.make_async_copy(of_bytes(sent + side), of_bytes(sent + side), send_sem).wait()
 
 
 def finish(sums_ref, log_rate_ref, state_ref, log_rate_out, state_out):
@@ -398,29 +429,29 @@
             pltpu.VMEM((members, rows), f32),
             pltpu.VMEM(col_basis.shape, bf16),
             pltpu.VMEM((3, members, rows), f32),
-            pltpu.VMEM(near_weight.shape, bf16),
+            pltpu.VMEM((3 * rows, half), bf16),
             pltpu.VMEM(coupling.shape, f32),
             pltpu.VMEM(factors.shape, f32),
-            pltpu.VMEM((levels, 2 * widest, group * 2 * widest), bf16),
+            pltpu.VMEM((rows, 2 * widest), bf16),
+            pltpu.VMEM((levels, group * 2 * widest, 2 * widest), bf16),
             pltpu.VMEM((4 * widest, rows), bf16),
             pltpu.VMEM((2, 2, members, half), bf16),
             pltpu.VMEM((2, 3, 2, members, half), bf16),
             pltpu.VMEM((2, n, members, 2 * widest), bf16),
             pltpu.VMEM((2, members, rows), f32),
             pltpu.VMEM((2, members, rows), f32),
-            pltpu.SemaphoreType.DMA((6,)),
+            pltpu.SemaphoreType.DMA((3,)),
             pltpu.SemaphoreType.REGULAR,
-            pltpu.SemaphoreType.DMA((2,)),
+            pltpu.SemaphoreType.REGULAR,
             pltpu.SemaphoreType.DMA,
             pltpu.SemaphoreType.DMA((2, 3)),
-            pltpu.SemaphoreType.DMA,
             pltpu.SemaphoreType.DMA((2, levels)),
             pltpu.SemaphoreType.DMA((2,)),
         ],
         compiler_params=pltpu.CompilerParams(
             collective_id=0, has_side_effects=True, vmem_limit_bytes=60 * 1024 * 1024
         ),
-    )(*args)
+    )(*args[:4], near_weight.reshape(3 * rows, half), *args[5:])
     return tuple(
         pl.pallas_call(
             finish,

time: 18.8 us -> 18.2 us (0.968)
  Pallas kernels: 17.3 us -> 16.7 us
    pallas_call x1, Pallas kernels: 16.7 us -> 16.1 us  [local(): pl.pallas_call(functools.partial(kernel, n, group), out_shape=pltpu.VMEM(...]
where the time goes in v2:
time: 18.2 us; the launch traced here: 18 us
  Pallas kernels  16.7 us (92%)
  between operations  1.33 us (7%)
    pallas_call x1, Pallas kernels, local(): pl.pallas_call(functools.partial(kernel, n, group), out_shape=pltpu.VMEM(...  16.1 us
    pallas_call x1, Pallas kernels, local(): pl.pallas_call(finish, out_shape=[jax.ShapeDtypeStruct((members, rows), f...  0.63 us

profile of v2, /device:TPU:0, one launch (start us, length us, event | category | flops | bytes accessed | tf_op | source)
XLA Modules:
  0.0 18.0 jit_solution(2278307333685431035)
XLA Ops:
  0.6 0.0 copy-start.1
  0.6 0.0 copy-start
  1.3 16.1 %shard_map.104.sums_ref = f32[2,8,1024]{2,1,0:T(8,128)S(1)} custom-call(f32[8,1024]{1,0:T(8,128)} %log_rate_ref.1, f32[8,1024]{1,0:T(8,128)} %state_ref.1, f32[8,1024]{1,0:T(8,128)} %rate_coef_hbm.1, f32[8,1024]{1,0:T(8,128)} %state_coef_hbm.1, bf16[3072,512]{1,0:T(8,128)(2,1)} %bitcast.1, bf16[64,1024]{1,0:T(8,128)(2,1)} %basis_hbm.1, ...), custom_call_target="tpu_custom_call" | custom-call | tf_op jit(solution)/shard_map/pallas_call | solution.py:423
  17.4 0.0 copy-done.1
  17.4 0.0 copy-done
  17.4 0.6 %shard_map.105 = (f32[8,1024]{1,0:T(8,128)}, f32[8,1024]{1,0:T(8,128)}) custom-call(f32[2,8,1024]{2,1,0:T(8,128)S(1)} %shard_map.104.sums_ref, f32[8,1024]{1,0:T(8,128)S(1)} %copy-done, f32[8,1024]{1,0:T(8,128)S(1)} %copy-done.1), custom_call_target="tpu_custom_call" | custom-call | tf_op jit(solution)/shard_map/pallas_call | solution.py:456
Async XLA Ops:
  0.6 16.7 %copy-start.1 = (f32[8,1024]{1,0:T(8,128)S(1)}, f32[8,1024]{1,0:T(8,128)}, u32[]{:S(2)}) copy-start(f32[8,1024]{1,0:T(8,128)} %state_ref.1) | copy-start | bytes 98308
  0.6 16.7 %copy-start = (f32[8,1024]{1,0:T(8,128)S(1)}, f32[8,1024]{1,0:T(8,128)}, u32[]{:S(2)}) copy-start(f32[8,1024]{1,0:T(8,128)} %log_rate_ref.1) | copy-start | bytes 98308

commit v3 on v2

--- a/solution.py
+++ b/solution.py
@@ -33,7 +33,7 @@
     coupling_hbm,
     factors_hbm,
     ranks_ref,
-    sums_out,
+    next_out,
     log_rate_ref,
     basis_ref,
     friction,
@@ -389,8 +389,8 @@
     stress_two, (state_two, healing, inverse) = rates(
         1, log_rate + step_length * rate_one, early_two
     )
-    sums_out[0] = rate_one + (stress_two - healing) * inverse
-    sums_out[1] = state_one + state_two
+    next_out[0] = log_rate + 0.5 * step_length * (rate_one + (stress_two - healing) * inverse)
+    next_out[1] = friction[0] + 0.5 * step_length * (state_one + state_two)
 
     sent = 2 * (n - 1) * members * 2 * widest * 2 + 2 * (members * half * 2 + members * rows * 4)
     side = 2 * 2 * members * half * 2
@@ -404,9 +404,15 @@
         pltpu.make_async_copy(of_bytes(sent + side), of_bytes(sent + side), send_sem).wait()
 
 
-def finish(sums_ref, log_rate_ref, state_ref, log_rate_out, state_out):
-    log_rate_out[...] = log_rate_ref[...] + 0.5 * step_length * sums_ref[0]
-    state_out[...] = state_ref[...] + 0.5 * step_length * sums_ref[1]
+def finish(next_ref, log_rate_out, state_out, sem):
+    copies = [
+        pltpu.make_async_copy(next_ref.at[i], target, sem.at[i])
+        for i, target in enumerate((log_rate_out, state_out))
+    ]
+    for copy in copies:
+        copy.start()
+    for copy in copies:
+        copy.wait()
 
 
 def local(n, *args):
@@ -420,7 +426,7 @@
     in_hbm = pl.BlockSpec(memory_space=pltpu.HBM)
     vmem = pl.BlockSpec(memory_space=pltpu.VMEM)
     smem = pl.BlockSpec(memory_space=pltpu.SMEM)
-    sums = pl.pallas_call(
+    both = pl.pallas_call(
         functools.partial(kernel, n, group),
         out_shape=pltpu.VMEM((2, members, rows), f32),
         in_specs=[in_hbm] * 8 + [smem],
@@ -456,10 +462,11 @@
         pl.pallas_call(
             finish,
             out_shape=[jax.ShapeDtypeStruct((members, rows), f32)] * 2,
-            in_specs=[vmem] * 3,
-            out_specs=[vmem] * 2,
+            in_specs=[vmem],
+            out_specs=[in_hbm] * 2,
+            scratch_shapes=[pltpu.SemaphoreType.DMA((2,))],
             compiler_params=pltpu.CompilerParams(vmem_limit_bytes=1024 * 1024),
-        )(sums, args[0], args[1])
+        )(both)
     )
 
 

time: 18.2 us -> 18.1 us (level)
  no operation moved by 1% of the time
where the time goes in v3:
time: 18.1 us; the launch traced here: 18 us
  Pallas kernels  16.7 us (92%)
  between operations  1.29 us (7%)
    pallas_call x1, Pallas kernels, local(): pl.pallas_call(functools.partial(kernel, n, group), out_shape=pltpu.VMEM(...  16.1 us
    pallas_call x1, Pallas kernels, local(): pl.pallas_call(finish, out_shape=[jax.ShapeDtypeStruct((members, rows), f...  0.65 us

profile of v3, /device:TPU:0, one launch (start us, length us, event | category | flops | bytes accessed | tf_op | source)
XLA Modules:
  0.0 18.0 jit_solution(8949008201248758851)
XLA Ops:
  1.3 16.1 %shard_map.104.next_ref = f32[2,8,1024]{2,1,0:T(8,128)S(1)} custom-call(f32[8,1024]{1,0:T(8,128)} %log_rate_hbm.1, f32[8,1024]{1,0:T(8,128)} %state_hbm.1, f32[8,1024]{1,0:T(8,128)} %rate_coef_hbm.1, f32[8,1024]{1,0:T(8,128)} %state_coef_hbm.1, bf16[3072,512]{1,0:T(8,128)(2,1)} %bitcast.1, bf16[64,1024]{1,0:T(8,128)(2,1)} %basis_hbm.1, ...), custom_call_target="tpu_custom_call" | custom-call | tf_op jit(solution)/shard_map/pallas_call | solution.py:429
  17.3 0.6 %shard_map.105 = (f32[8,1024]{1,0:T(8,128)}, f32[8,1024]{1,0:T(8,128)}) custom-call(f32[2,8,1024]{2,1,0:T(8,128)S(1)} %shard_map.104.next_ref), custom_call_target="tpu_custom_call" | custom-call | tf_op jit(solution)/shard_map/pallas_call | solution.py:462
